TPU v7x, 32 devices: a whole 2x2x4 slice. The times are simulated.
32 devices in a mesh: grp: 2 (over y), seq: 4 (over z), zero: 4 (over x, core).
Axes of the slice: x: 2, y: 2, z: 4, core: 2. Of those that a mesh axis runs over, the one named last changes fastest.
Arguments:
- hidden: bfloat16 [8, 512, 1280], P(('grp', 'zero'), 'seq'), parts along dimension 0, may hold values from -6 to 6
- grad_out: bfloat16 [8, 512, 1280], P(('grp', 'zero'), 'seq'), parts along dimension 0, may hold values from -6 to 6
- w_proj: bfloat16 [1280, 148], P('zero'), may hold values from -0.15625 to 0.15625
- conv_w: bfloat16 [4, 1408], P(None, 'zero'), may hold values from -3 to 3
- a_log: float32 [20], replicated, may hold values from -8 to 1, as said below
- dt_bias: float32 [20], replicated, may hold values from -4.5 to -3
Outputs:
- output: bfloat16 [8, 512, 1280], P(('grp', 'zero'), 'seq'), parts along dimension 0
- grad_hidden: bfloat16 [8, 512, 1280], P(('grp', 'zero'), 'seq'), parts along dimension 0
- grad_proj: float32 [2560, 148], P(('grp', 'zero')), parts along dimension 0
- grad_conv: float32 [8, 1408], P('grp', 'zero'), parts along dimension 0
- grad_heads: float32 [4, 20], P('grp'), parts along dimension 0
There are 2 independent parts, one for each index of `grp`. A program takes and returns all parts, laid end to end along the dimension named above; an argument that names none is the same for every part. Nothing has to cross between parts.
Inputs may be any that keep to these rules, and one draw needn't show every extreme that they name: `a_log`: the logarithms of the heads' decay rates.
All inputs are finite; a program needn't handle non-finite values.
Results may differ from a plain program's by a relative error of at most 0.017.
Values may be sent and summed in bfloat16 or wider, within the bound.
A program may use at most 192 MiB of HBM per device.

v0:
```python
import jax
import jax.numpy as jnp
from jax import lax
from jax.sharding import PartitionSpec as P

WIDTH = 1280
STATE = 64
HEAD_DIM = 64
SPAN = 128
KERNEL = 4


def prefix(x, axis, join, neutral, backward):
    count = lax.axis_size(axis)
    place = lax.axis_index(axis)
    ahead = count - 1 - place if backward else place
    gathered = jax.tree.map(
        lambda a, kind: lax.all_gather(a.astype(kind), axis),
        x,
        jax.tree.map(lambda a: jnp.bfloat16 if a.dtype == jnp.float32 else a.dtype, x),
    )
    state = jax.tree.map(lambda a, e: jnp.zeros_like(a) + jnp.asarray(e, a.dtype), x, neutral)

    def one(hop, state):
        source = count - 1 - hop if backward else hop
        return join(
            state,
            jax.tree.map(
                lambda a, own: lax.dynamic_index_in_dim(a, source, 0, False).astype(own.dtype),
                gathered,
                x,
            ),
        )

    return lax.fori_loop(0, ahead, one, state)


def extended(x, sides, width):
    for axis, dim in sides:
        size, length = (lax.axis_size(axis), x.shape[dim])
        up = [(i, (i + 1) % size) for i in range(size - 1)]
        down = [(j, i) for i, j in up]
        last = lax.slice_in_dim(x, length - width, length, axis=dim)
        leading = lax.slice_in_dim(x, 0, width, axis=dim)
        before = lax.ppermute(last, axis, up)
        after = lax.ppermute(leading, axis, down)
        x = jnp.concatenate([before, x, after], axis=dim)
    return x


def combine_states(earlier, later):
    return (earlier[0] * later[0], later[0][..., None, None] * earlier[1] + later[1])


def pass_upward(pieces):
    identity = (jnp.ones_like(pieces[0]), jnp.zeros_like(pieces[1]))
    return prefix(pieces, "seq", combine_states, identity, False)[1]


def pass_downward(pieces):
    identity = (jnp.ones_like(pieces[0]), jnp.zeros_like(pieces[1]))
    return prefix(pieces, "seq", combine_states, identity, True)[1]


def conv_core(ahead_in, dt_raw, filters, a_log, dt_bias):
    length = dt_raw.shape[0]
    head_count = dt_raw.shape[1]
    blocks = length // SPAN
    mixed_sum = filters[0] * ahead_in[KERNEL - 1 : KERNEL - 1 + length]
    for step_back in range(1, KERNEL):
        mixed_sum = (
            mixed_sum
            + filters[step_back]
            * ahead_in[KERNEL - 1 - step_back : KERNEL - 1 - step_back + length]
        )
    active = jax.nn.silu(mixed_sum)
    values = active[:, :WIDTH].astype(jnp.bfloat16).reshape(blocks, SPAN, head_count, HEAD_DIM)
    b_mat = active[:, WIDTH : WIDTH + STATE].astype(jnp.bfloat16).reshape(blocks, SPAN, STATE)
    c_mat = active[:, WIDTH + STATE :].astype(jnp.bfloat16)
    c_blocks = c_mat.reshape(blocks, SPAN, STATE)
    steps_dt = jax.nn.softplus(dt_raw + dt_bias)
    log_decay = -jnp.exp(a_log) * steps_dt
    within = jnp.cumsum(log_decay.reshape(blocks, SPAN, head_count), axis=1).transpose(0, 2, 1)
    dt_blocks = steps_dt.reshape(blocks, SPAN, head_count).transpose(0, 2, 1)
    scores = jnp.einsum("kin,kjn->kij", c_blocks, b_mat, preferred_element_type=jnp.float32)
    causal = jnp.arange(SPAN)[:, None] >= jnp.arange(SPAN)[None, :]
    gap_log = within[:, :, :, None] - within[:, :, None, :]
    decays = jnp.exp(jnp.where(causal, gap_log, -jnp.inf))
    weights = (scores[:, None] * decays * dt_blocks[:, :, None, :]).astype(jnp.bfloat16)
    y_intra = jnp.einsum("khij,kjhp->kihp", weights, values, preferred_element_type=jnp.float32)
    to_end = jnp.exp(within[:, :, -1:] - within) * dt_blocks
    b_weighted = (to_end[..., None] * b_mat[:, None, :, :].astype(jnp.float32)).astype(jnp.bfloat16)
    states = jnp.einsum("khjn,kjhp->khnp", b_weighted, values, preferred_element_type=jnp.float32)
    totals = within[:, :, -1]

    def advance(carried, current):
        return (jnp.exp(current[0])[:, None, None] * carried + current[1], carried)

    last_state, entering = lax.scan(
        advance, jnp.zeros(states.shape[1:], jnp.float32), (totals, states)
    )
    y_inter = jnp.einsum(
        "kin,khnp->kihp", c_blocks.astype(jnp.float32), entering, precision=lax.Precision.HIGH
    )
    y_inter = y_inter * jnp.exp(within).transpose(0, 2, 1)[..., None]
    y_local = (y_intra + y_inter).reshape(length, WIDTH)
    offsets = jnp.cumsum(totals, axis=0) - totals
    reached = jnp.exp(within + offsets[:, :, None]).transpose(0, 2, 1).reshape(length, head_count)
    overall = jnp.exp(jnp.sum(totals, axis=0))
    return (y_local, overall, last_state, reached, c_mat)


def add_incoming(y_local, reached, c_mat, incoming):
    carried = jnp.einsum(
        "tn,hnp->thp", c_mat.astype(jnp.float32), incoming, precision=lax.Precision.HIGH
    )
    return y_local + (reached[:, :, None] * carried).reshape(y_local.shape)


def strand_pass(tokens, cotangent, w_full, filters, a_log, dt_bias):
    length = tokens.shape[1]
    margin = KERNEL - 1
    projected = jnp.einsum("std,dc->stc", tokens, w_full, preferred_element_type=jnp.float32)
    inner_act = jnp.concatenate([tokens, projected[..., : 2 * STATE].astype(jnp.bfloat16)], axis=2)
    dt_raw = projected[..., 2 * STATE :]
    padded = extended(inner_act, (("seq", 1),), margin)
    padded = padded.astype(jnp.float32)
    ahead_in = padded[:, : length + margin]
    behind = jnp.flip(padded[:, margin:], axis=1)
    core_batch = jax.vmap(conv_core, in_axes=(0, 0, None, None, None))
    finish_batch = jax.vmap(add_incoming)
    ahead_out, ahead_back = jax.vjp(core_batch, ahead_in, dt_raw, filters, a_log, dt_bias)
    behind_out, behind_back = jax.vjp(
        core_batch, behind, jnp.flip(dt_raw, axis=1), filters, a_log, dt_bias
    )
    ahead_state = pass_upward((ahead_out[1], ahead_out[2]))
    behind_state = pass_downward((behind_out[1], behind_out[2]))
    y_ahead, ahead_finish = jax.vjp(
        finish_batch, ahead_out[0], ahead_out[3], ahead_out[4], ahead_state
    )
    y_behind, behind_finish = jax.vjp(
        finish_batch, behind_out[0], behind_out[3], behind_out[4], behind_state
    )
    result = (y_ahead + jnp.flip(y_behind, axis=1)).astype(jnp.bfloat16)
    upstream = cotangent.astype(jnp.float32)
    grad_ahead = ahead_finish(upstream)
    grad_behind = behind_finish(jnp.flip(upstream, axis=1))
    later_ahead = pass_downward((ahead_out[1], grad_ahead[3]))
    later_behind = pass_upward((behind_out[1], grad_behind[3]))
    core_ahead = ahead_back(
        (
            grad_ahead[0],
            jnp.sum(later_ahead * ahead_state, axis=(-2, -1)),
            later_ahead,
            grad_ahead[1],
            grad_ahead[2],
        )
    )
    core_behind = behind_back(
        (
            grad_behind[0],
            jnp.sum(later_behind * behind_state, axis=(-2, -1)),
            later_behind,
            grad_behind[1],
            grad_behind[2],
        )
    )
    grad_padded = jnp.pad(core_ahead[0], ((0, 0), (0, margin), (0, 0))) + jnp.pad(
        jnp.flip(core_behind[0], axis=1), ((0, 0), (margin, 0), (0, 0))
    )
    rims = jnp.concatenate([grad_padded[:, :margin], grad_padded[:, length + margin :]], axis=1)
    rims = extended(rims.astype(jnp.bfloat16), (("seq", 1),), margin).astype(rims.dtype)
    own_rows = grad_padded[:, margin : length + margin]
    own_rows = own_rows.at[:, :margin].add(rims[:, :margin])
    own_rows = own_rows.at[:, length - margin :].add(rims[:, 3 * margin :])
    grad_inner = own_rows.astype(jnp.bfloat16)
    grad_dt = core_ahead[1] + jnp.flip(core_behind[1], axis=1)
    grad_projected = jnp.concatenate(
        [grad_inner[..., WIDTH:], grad_dt.astype(jnp.bfloat16)], axis=2
    )
    grad_weight = jnp.einsum(
        "std,stc->dc", tokens, grad_projected, preferred_element_type=jnp.float32
    )
    back_proj = jnp.einsum(
        "stc,dc->std", grad_projected, w_full, preferred_element_type=jnp.float32
    )
    grad_tokens = (grad_inner[..., :WIDTH].astype(jnp.float32) + back_proj).astype(jnp.bfloat16)
    grad_filters = core_ahead[2] + core_behind[2]
    grad_decay = jnp.stack([core_ahead[3] + core_behind[3], core_ahead[4] + core_behind[4]])
    return (result, grad_tokens, grad_weight, grad_filters, grad_decay)


def per_device(hidden, grad_out, w_proj, conv_w, a_log, dt_bias):
    w_full, conv_full = (
        lax.all_gather(w_proj, "zero", axis=0, tiled=True),
        lax.all_gather(conv_w, "zero", axis=1, tiled=True),
    )
    filters = conv_full.astype(jnp.float32)
    first = strand_pass(hidden, grad_out, w_full, filters, a_log, dt_bias)
    second = strand_pass(
        jnp.flip(hidden, axis=2), jnp.flip(grad_out, axis=2), w_full, filters, a_log, dt_bias
    )
    first_out, first_grad = (first[0], first[1])
    other_out = jnp.flip(second[0], axis=2)
    other_grad = jnp.flip(second[1], axis=2)
    grad_weight = first[2] + second[2]
    grad_filters = first[3] + second[3]
    grad_decay = first[4] + second[4]
    output = (first_out.astype(jnp.float32) + other_out.astype(jnp.float32)).astype(jnp.bfloat16)
    grad_hidden = (first_grad.astype(jnp.float32) + other_grad.astype(jnp.float32)).astype(
        jnp.bfloat16
    )
    part_weight, part_filters = (
        lax.psum_scatter(
            grad_weight.astype(jnp.bfloat16), "zero", scatter_dimension=0, tiled=True
        ).astype(jnp.float32),
        lax.psum_scatter(
            grad_filters.astype(jnp.bfloat16), "zero", scatter_dimension=1, tiled=True
        ).astype(jnp.float32),
    )
    share_weight, share_filters = (
        lax.psum(part_weight.astype(jnp.bfloat16), "seq").astype(jnp.float32),
        lax.psum(part_filters.astype(jnp.bfloat16), "seq").astype(jnp.float32),
    )
    grad_heads = lax.psum(grad_decay, ("seq", "zero"))
    return (output, grad_hidden, share_weight, share_filters, grad_heads)


def solution(mesh):
    return jax.shard_map(
        per_device,
        mesh=mesh,
        in_specs=(
            P(("grp", "zero"), "seq", None),
            P(("grp", "zero"), "seq", None),
            P("zero", None),
            P(None, "zero"),
            P(),
            P(),
        ),
        out_specs=(
            P(("grp", "zero"), "seq", None),
            P(("grp", "zero"), "seq", None),
            P(("grp", "zero"), None),
            P("grp", "zero"),
            P("grp", None),
        ),
        check_vma=False,
    )
```

profile of v0, /device:TPU:0, one launch (start us, length us, event | category | flops | bytes accessed | tf_op | source)
XLA Modules:
  0.0 792.8 jit_solution(859587964172044816)
XLA Ops:
  7.2 8.7 %all-gather.13 = bf16[4,320,148]{1,2,0:T(8,128)(2,1)S(1)} all-gather(bf16[1,320,148]{1,2,0:T(8,128)(2,1)} %bitcast.1260), channel_id=1, replica_groups=mesh['grp'=2,'seq'=4,'zero'=4] {'zero'}, dimensions={0}, use_global_device_ids=true | all-gather | bytes 473600 | tf_op jit(solution)/shard_map/all_gather | solution.py:195
  62.5 9.1 %all-gather.6 = bf16[4,1,20,1]{2,3,1,0:T(2,128)(2,1)} all-gather(bf16[1,1,20,1]{2,3,1,0:T(2,128)(2,1)S(1)} %get-tuple-element.1334), channel_id=8, replica_groups=mesh['grp'=2,'seq'=4,'zero'=4] {'seq'}, dimensions={0}, use_global_device_ids=true | all-gather | bytes 200 | tf_op jit(solution)/shard_map/all_gather | solution.py:18
  71.6 8.6 %all-gather.4 = bf16[4,1,20,1]{2,3,1,0:T(2,128)(2,1)} all-gather(bf16[1,1,20,1]{2,3,1,0:T(2,128)(2,1)S(1)} %get-tuple-element.1331), channel_id=6, replica_groups=mesh['grp'=2,'seq'=4,'zero'=4] {'seq'}, dimensions={0}, use_global_device_ids=true | all-gather | bytes 200 | tf_op jit(solution)/shard_map/all_gather | solution.py:18
  80.2 8.9 %all-gather.2 = bf16[4,1,20,1]{2,3,1,0:T(2,128)(2,1)} all-gather(bf16[1,1,20,1]{2,3,1,0:T(2,128)(2,1)S(1)} %get-tuple-element.1328), channel_id=4, replica_groups=mesh['grp'=2,'seq'=4,'zero'=4] {'seq'}, dimensions={0}, use_global_device_ids=true | all-gather | bytes 200 | tf_op jit(solution)/shard_map/all_gather | solution.py:18
  89.2 8.9 %all-gather = bf16[4,1,20,1]{2,3,1,0:T(2,128)(2,1)} all-gather(bf16[1,1,20,1]{2,3,1,0:T(2,128)(2,1)S(1)} %get-tuple-element.1325), channel_id=2, replica_groups=mesh['grp'=2,'seq'=4,'zero'=4] {'seq'}, dimensions={0}, use_global_device_ids=true | all-gather | bytes 200 | tf_op jit(solution)/shard_map/all_gather | solution.py:18
  157.0 6.6 slice.366
  174.2 19.9 %all-gather.7 = bf16[80,64,64]{2,1,0:T(8,128)(2,1)} all-gather(bf16[20,64,64]{2,1,0:T(8,128)(2,1)S(1)} %fusion.28), channel_id=9, replica_groups=mesh['grp'=2,'seq'=4,'zero'=4] {'seq'}, dimensions={0}, use_global_device_ids=true | all-gather | bytes 819200 | tf_op jit(solution)/shard_map/all_gather | solution.py:18
  203.9 19.0 %all-gather.11 = bf16[4,20,64,64]{3,2,1,0:T(8,128)(2,1)} all-gather(bf16[1,20,64,64]{3,2,1,0:T(8,128)(2,1)} %copy.689), channel_id=13, replica_groups=mesh['grp'=2,'seq'=4,'zero'=4] {'seq'}, dimensions={0}, use_global_device_ids=true | all-gather | bytes 819200 | tf_op jit(solution)/shard_map/all_gather | solution.py:18
  239.3 24.0 %all-gather.3 = bf16[80,64,64]{2,1,0:T(8,128)(2,1)} all-gather(bf16[20,64,64]{2,1,0:T(8,128)(2,1)S(1)} %fusion.26), channel_id=5, replica_groups=mesh['grp'=2,'seq'=4,'zero'=4] {'seq'}, dimensions={0}, use_global_device_ids=true | all-gather | bytes 819200 | tf_op jit(solution)/shard_map/all_gather | solution.py:18
  264.2 8.3 %while.69 = (s32[]{:T(128)}, f32[1,20,64,64]{3,2,1,0:T(8,128)}, s32[]{:T(128)}, bf16[4,1,20]{2,1,0:T(2,128)(2,1)}, bf16[4,1,20,64,64]{4,3,2,1,0:T(8,128)(2,1)}, ...) while((s32[]{:T(128)}, f32[1,20,64,64]{3,2,1,0:T(8,128)}, s32[]{:T(128)}, bf16[4,1,20]{2,1,0:T(2,128)(2,1)}, ...), condition=%wide.region_5.7_spmd, body=%wide.region_4.6_spmd.sunk | while | flops 245786 | bytes 819555 | solution.py:35
  276.5 19.0 %all-gather.9 = bf16[4,20,64,64]{3,2,1,0:T(8,128)(2,1)} all-gather(bf16[1,20,64,64]{3,2,1,0:T(8,128)(2,1)} %copy.664), channel_id=11, replica_groups=mesh['grp'=2,'seq'=4,'zero'=4] {'seq'}, dimensions={0}, use_global_device_ids=true | all-gather | bytes 819200 | tf_op jit(solution)/shard_map/all_gather | solution.py:18
  340.2 29.1 %all-gather.10 = bf16[4,20,64,64]{3,2,1,0:T(8,128)(2,1)} all-gather(bf16[1,20,64,64]{3,2,1,0:T(8,128)(2,1)} %copy.684), channel_id=12, replica_groups=mesh['grp'=2,'seq'=4,'zero'=4] {'seq'}, dimensions={0}, use_global_device_ids=true | all-gather | bytes 819200 | tf_op jit(solution)/shard_map/all_gather | solution.py:18
  370.3 8.5 %while.74 = (s32[]{:T(128)}, f32[1,20,64,64]{3,2,1,0:T(8,128)}, s32[]{:T(128)}, bf16[4,1,20]{2,1,0:T(2,128)(2,1)}, bf16[4,1,20,64,64]{4,3,2,1,0:T(8,128)(2,1)}, ...) while((s32[]{:T(128)}, f32[1,20,64,64]{3,2,1,0:T(8,128)}, s32[]{:T(128)}, bf16[4,1,20]{2,1,0:T(2,128)(2,1)}, ...), condition=%wide.region_44.46_spmd, body=%wide.region_43.45_spmd.sunk | while | flops 245786 | bytes 819555 | solution.py:35
  393.5 21.7 %all-gather.8 = bf16[4,20,64,64]{3,2,1,0:T(8,128)(2,1)} all-gather(bf16[1,20,64,64]{3,2,1,0:T(8,128)(2,1)} %copy.659), channel_id=10, replica_groups=mesh['grp'=2,'seq'=4,'zero'=4] {'seq'}, dimensions={0}, use_global_device_ids=true | all-gather | bytes 819200 | tf_op jit(solution)/shard_map/all_gather | solution.py:18
  416.1 8.3 %while.72 = (s32[]{:T(128)}, f32[1,20,64,64]{3,2,1,0:T(8,128)}, s32[]{:T(128)}, bf16[4,1,20]{2,1,0:T(2,128)(2,1)}, bf16[4,1,20,64,64]{4,3,2,1,0:T(8,128)(2,1)}, ...) while((s32[]{:T(128)}, f32[1,20,64,64]{3,2,1,0:T(8,128)}, s32[]{:T(128)}, bf16[4,1,20]{2,1,0:T(2,128)(2,1)}, ...), condition=%wide.region_14.16_spmd, body=%wide.region_13.15_spmd.sunk | while | flops 245786 | bytes 819555 | solution.py:35
  429.0 23.8 %all-gather.5 = bf16[80,64,64]{2,1,0:T(8,128)(2,1)} all-gather(bf16[20,64,64]{2,1,0:T(8,128)(2,1)S(1)} %fusion.27), channel_id=7, replica_groups=mesh['grp'=2,'seq'=4,'zero'=4] {'seq'}, dimensions={0}, use_global_device_ids=true | all-gather | bytes 819200 | tf_op jit(solution)/shard_map/all_gather | solution.py:18
  455.1 26.7 %all-gather.1 = bf16[80,64,64]{2,1,0:T(8,128)(2,1)} all-gather(bf16[20,64,64]{2,1,0:T(8,128)(2,1)S(1)} %fusion.25), channel_id=3, replica_groups=mesh['grp'=2,'seq'=4,'zero'=4] {'seq'}, dimensions={0}, use_global_device_ids=true | all-gather | bytes 819200 | tf_op jit(solution)/shard_map/all_gather | solution.py:18
  507.1 8.0 %reverse.8 = f32[1,256,1408]{1,2,0:T(8,128)} reverse(f32[1,256,1408]{1,2,0:T(8,128)S(1)} %bitcast.1187), dimensions={1} | reverse | bytes 2883584
  525.7 12.4 %reverse.9 = f32[1,256,1408]{1,2,0:T(8,128)} reverse(f32[1,256,1408]{1,2,0:T(8,128)} %bitcast.1188), dimensions={1} | reverse | bytes 2883584
  570.1 6.8 collective-permute-start.6
  697.5 31.7 %psum.23 = f32[2,20]{1,0:T(2,128)} all-reduce(f32[2,20]{1,0:T(2,128)S(1)} %maximum_add_fusion), channel_id=1, replica_groups=mesh['grp'=2,'seq'=4,'zero'=4] {'seq','zero'}, use_global_device_ids=true, to_apply=%region_100.102 | all-reduce | flops 40 | bytes 320 | tf_op jit(solution)/shard_map/psum | solution.py:225
  735.0 12.3 %reduce-scatter.9.cloned.1.call-done = bf16[352,4]{1,0:T(8,128)(2,1)} async-done(((bf16[1408,4]{1,0:T(8,128)(2,1)}), bf16[352,4]{1,0:T(8,128)(2,1)}) %reduce-scatter.9.cloned.1.call-update) | async-done | bytes 2832
  748.3 11.7 %psum.22 = bf16[4,352]{1,0:T(4,128)(2,1)S(1)} all-reduce(bf16[4,352]{1,0:T(4,128)(2,1)S(1)} %copy.719), channel_id=1, replica_groups=mesh['grp'=2,'seq'=4,'zero'=4] {'seq'}, use_global_device_ids=true, to_apply=%region_91.93 | all-reduce | flops 1408 | bytes 5632 | tf_op jit(solution)/shard_map/psum | solution.py:223
  760.6 23.9 %all-reduce.58.cloned.1.call-done = bf16[320,148]{0,1:T(8,128)(2,1)} async-done(((bf16[320,148]{0,1:T(8,128)(2,1)}), bf16[320,148]{0,1:T(8,128)(2,1)}) %all-reduce.58.cloned.1.call-update) | async-done | bytes 94736 | tf_op jit(solution)/shard_map/psum | solution.py:222
  (858 shorter events, 440.1 us)
Async XLA Ops:
  7.2 724.8 %reduce-scatter.7.cloned.1.call-start = ((), (), s32[]{:S(2)}) async-start(), calls=%async_computation.3 | async-start | bytes 819200
  18.1 106.2 %collective-permute-start.1 = (bf16[1,3,1408]{1,2,0:T(8,128)(2,1)}, bf16[1,3,1408]{1,2,0:T(8,128)(2,1)}, u32[]{:S(2)}, u32[]{:S(2)}) collective-permute-start(bf16[1,3,1408]{1,2,0:T(8,128)(2,1)} %get-tuple-element.1305), channel_id=1, source_target_pairs={{4,0},{8,4},{12,8},{5,1},{9,5},{13,9},{6,2},{10,6},{14,10},{7,3},{... | collective-permute-start | bytes 25352 | tf_op jit(solution)/shard_map/ppermute | solution.py:46
  19.4 104.9 %collective-permute-start = (bf16[1,3,1408]{1,2,0:T(8,128)(2,1)}, bf16[1,3,1408]{1,2,0:T(8,128)(2,1)}, u32[]{:S(2)}, u32[]{:S(2)}) collective-permute-start(bf16[1,3,1408]{1,2,0:T(8,128)(2,1)} %get-tuple-element.1304), channel_id=1, source_target_pairs={{0,4},{4,8},{8,12},{1,5},{5,9},{9,13},{2,6},{6,10},{10,14},{3,7},{... | collective-permute-start | bytes 25352 | tf_op jit(solution)/shard_map/ppermute | solution.py:45
  25.1 73.0 %copy-start.25 = (bf16[1,128,1280]{1,2,0:T(8,128)(2,1)}, bf16[1,128,1280]{1,2,0:T(8,128)(2,1)S(1)}, u32[]{:S(2)}) copy-start(bf16[1,128,1280]{1,2,0:T(8,128)(2,1)S(1)} %rev.50) | copy-start | bytes 983044
  26.6 71.6 %collective-permute-start.3 = (bf16[1,3,1408]{1,2,0:T(8,128)(2,1)}, bf16[1,3,1408]{1,2,0:T(8,128)(2,1)}, u32[]{:S(2)}, u32[]{:S(2)}) collective-permute-start(bf16[1,3,1408]{1,2,0:T(8,128)(2,1)} %get-tuple-element.1307), channel_id=1, source_target_pairs={{4,0},{8,4},{12,8},{5,1},{9,5},{13,9},{6,2},{10,6},{14,10},{7,3},{... | collective-permute-start | bytes 25352 | tf_op jit(solution)/shard_map/ppermute | solution.py:46
  27.9 70.3 %collective-permute-start.2 = (bf16[1,3,1408]{1,2,0:T(8,128)(2,1)}, bf16[1,3,1408]{1,2,0:T(8,128)(2,1)}, u32[]{:S(2)}, u32[]{:S(2)}) collective-permute-start(bf16[1,3,1408]{1,2,0:T(8,128)(2,1)} %get-tuple-element.1306), channel_id=1, source_target_pairs={{0,4},{4,8},{8,12},{1,5},{5,9},{9,13},{2,6},{6,10},{10,14},{3,7},{... | collective-permute-start | bytes 25352 | tf_op jit(solution)/shard_map/ppermute | solution.py:45
  33.6 23.5 %copy-start.52 = (f32[1,1,128,20]{3,2,1,0:T(8,128)}, f32[1,1,128,20]{3,2,1,0:T(8,128)S(1)}, u32[]{:S(2)}) copy-start(f32[1,1,128,20]{3,2,1,0:T(8,128)S(1)} %reduce_window_sum.90) | copy-start | bytes 30724
  35.8 24.7 %copy-start.54 = (f32[1,1,128,20]{3,2,1,0:T(8,128)}, f32[1,1,128,20]{3,2,1,0:T(8,128)S(1)}, u32[]{:S(2)}) copy-start(f32[1,1,128,20]{3,2,1,0:T(8,128)S(1)} %reduce_window_sum.86) | copy-start | bytes 30724
  37.2 21.9 %copy-start.56 = (f32[1,1,128,20]{3,2,1,0:T(8,128)}, f32[1,1,128,20]{3,2,1,0:T(8,128)S(1)}, u32[]{:S(2)}) copy-start(f32[1,1,128,20]{3,2,1,0:T(8,128)S(1)} %reduce_window_sum.88) | copy-start | bytes 30724
  38.6 22.6 %copy-start.58 = (f32[1,1,128,20]{3,2,1,0:T(8,128)}, f32[1,1,128,20]{3,2,1,0:T(8,128)S(1)}, u32[]{:S(2)}) copy-start(f32[1,1,128,20]{3,2,1,0:T(8,128)S(1)} %reduce_window_sum.84) | copy-start | bytes 30724
  45.0 80.9 %copy-start.140 = (f32[1408]{0:T(1024)}, f32[1408]{0:T(1024)S(1)}, u32[]{:S(2)}) copy-start(f32[1408]{0:T(1024)S(1)} %get-tuple-element.1150) | copy-start | bytes 16900
  45.1 80.9 %copy-start.142 = (f32[1408]{0:T(1024)}, f32[1408]{0:T(1024)S(1)}, u32[]{:S(2)}) copy-start(f32[1408]{0:T(1024)S(1)} %get-tuple-element.1151) | copy-start | bytes 16900
  199.6 23.3 %copy-start.2 = (f32[1,20,64,64]{3,2,1,0:T(8,128)}, f32[1,20,64,64]{3,2,1,0:T(8,128)S(1)}, u32[]{:S(2)}) copy-start(f32[1,20,64,64]{3,2,1,0:T(8,128)S(1)} %get-tuple-element.760) | copy-start | bytes 983044
  568.8 93.1 %collective-permute-start.7 = (bf16[1,3,1408]{1,2,0:T(8,128)(2,1)}, bf16[1,3,1408]{1,2,0:T(8,128)(2,1)}, u32[]{:S(2)}, u32[]{:S(2)}) collective-permute-start(bf16[1,3,1408]{1,2,0:T(8,128)(2,1)} %get-tuple-element.1271), channel_id=1, source_target_pairs={{4,0},{8,4},{12,8},{5,1},{9,5},{13,9},{6,2},{10,6},{14,10},{7,3},{... | collective-permute-start | bytes 25352 | tf_op jit(solution)/shard_map/ppermute | solution.py:46
  570.1 91.8 %collective-permute-start.6 = (bf16[1,3,1408]{1,2,0:T(8,128)(2,1)}, bf16[1,3,1408]{1,2,0:T(8,128)(2,1)}, u32[]{:S(2)}, u32[]{:S(2)}) collective-permute-start(bf16[1,3,1408]{1,2,0:T(8,128)(2,1)} %get-tuple-element.1270), channel_id=1, source_target_pairs={{0,4},{4,8},{8,12},{1,5},{5,9},{9,13},{2,6},{6,10},{10,14},{3,7},{... | collective-permute-start | bytes 25352 | tf_op jit(solution)/shard_map/ppermute | solution.py:45
  589.2 21.5 %copy-start.123 = (f32[1,1,128,20]{3,2,1,0:T(8,128)}, f32[1,1,128,20]{3,2,1,0:T(8,128)S(1)}, u32[]{:S(2)}) copy-start(f32[1,1,128,20]{3,2,1,0:T(8,128)S(1)} %reduce_window_sum.95) | copy-start | bytes 30724
  591.2 86.8 %collective-permute-start.5 = (bf16[1,3,1408]{1,2,0:T(8,128)(2,1)}, bf16[1,3,1408]{1,2,0:T(8,128)(2,1)}, u32[]{:S(2)}, u32[]{:S(2)}) collective-permute-start(bf16[1,3,1408]{1,2,0:T(8,128)(2,1)} %get-tuple-element.1269), channel_id=1, source_target_pairs={{4,0},{8,4},{12,8},{5,1},{9,5},{13,9},{6,2},{10,6},{14,10},{7,3},{... | collective-permute-start | bytes 25352 | tf_op jit(solution)/shard_map/ppermute | solution.py:46
  592.5 85.5 %collective-permute-start.4 = (bf16[1,3,1408]{1,2,0:T(8,128)(2,1)}, bf16[1,3,1408]{1,2,0:T(8,128)(2,1)}, u32[]{:S(2)}, u32[]{:S(2)}) collective-permute-start(bf16[1,3,1408]{1,2,0:T(8,128)(2,1)} %get-tuple-element.1268), channel_id=1, source_target_pairs={{0,4},{4,8},{8,12},{1,5},{5,9},{9,13},{2,6},{6,10},{10,14},{3,7},{... | collective-permute-start | bytes 25352 | tf_op jit(solution)/shard_map/ppermute | solution.py:45
  639.3 24.9 %copy-start.14 = (f32[1,131,1408]{1,2,0:T(8,128)S(1)}, f32[1,131,1408]{1,2,0:T(8,128)}, u32[]{:S(2)}) copy-start(f32[1,131,1408]{1,2,0:T(8,128)} %copy-done.13) | copy-start | bytes 2213380
  695.0 34.3 %copy-start.88 = (f32[1,128,1280]{2,1,0:T(8,128)S(1)}, f32[1,128,1280]{2,1,0:T(8,128)}, u32[]{:S(2)}) copy-start(f32[1,128,1280]{2,1,0:T(8,128)} %rev.49) | copy-start | bytes 1966084
  695.0 34.3 %copy-start.89 = (f32[1,128,1280]{2,1,0:T(8,128)S(1)}, f32[1,128,1280]{2,1,0:T(8,128)}, u32[]{:S(2)}) copy-start(f32[1,128,1280]{2,1,0:T(8,128)} %copy.618) | copy-start | bytes 1966084
  695.0 34.3 %copy-start.90 = (f32[1,128,1280]{2,1,0:T(8,128)S(1)}, f32[1,128,1280]{2,1,0:T(8,128)}, u32[]{:S(2)}) copy-start(f32[1,128,1280]{2,1,0:T(8,128)} %copy.619) | copy-start | bytes 1966084
  696.1 51.2 %reduce-scatter.9.cloned.1.call-start = ((), (), s32[]{:S(2)}) async-start(), calls=%async_computation.4 | async-start | bytes 450560
  729.2 55.2 %all-reduce.58.cloned.1.call-start = ((), (), s32[]{:S(2)}) async-start(), calls=%async_computation.2 | async-start | bytes 233472 | tf_op jit(solution)/shard_map/psum | solution.py:222
  (246 other events, 1305.6 us)
Sparse Core Ops, SparseCore 0:
  696.3 26.8 reduce-scatter.6
  729.4 17.9 reduce-scatter.8
  750.3 34.0 all-reduce.57
where the time goes:
time: 808 us; the launch traced here: 793 us
  blocking collectives  276 us (34%)
  local copies, waits for them, and re-layouts  219 us (27%)
  other arithmetic  139 us (17%)
  matrix products  75.8 us (9%)
  waiting for transfers between devices  36.3 us (4%)
  starting transfers between devices  28.9 us (4%)
  between operations  17 us (2%)
    all_gather x12, blocking collectives, prefix(): lax.all_gather(a.astype(kind), axis)  219 us
    unnamed x530, local copies, waits for them, and re-layouts  38.1 us
    slice x6, local copies, waits for them, and re-layouts, conv_core(): ahead_in[KERNEL - 1 - step_back:KERNEL - 1 - step_back + length]  37.1 us
    psum x1, blocking collectives, per_device(): grad_heads = lax.psum(grad_decay, ('seq', 'zero'))  31.7 us
    psum x1, waiting for transfers between devices, per_device(): lax.psum(part_weight.astype(jnp.bfloat16), 'seq').astype(jnp.float32)  23.9 us
    ppermute x4, starting transfers between devices, extended(): before = lax.ppermute(last, axis, up)  23.6 us
    add x12, other arithmetic, combine_states(): later[0][..., None, None] * earlier[1] + later[1]  22.9 us
    dot_general x12, matrix products, conv_core(): jnp.einsum('khij,kjhp->kihp', weights, values, preferred_element_type=jnp...  20.9 us
  transfers between devices with their start and end apart: 11, of which 2 were waited for; matrix products, arithmetic and copies ran while one was open for 19% of the time, Pallas kernels for 0%

commit v1 on v0

--- a/solution.py
+++ b/solution.py
@@ -219,7 +219,9 @@
         ).astype(jnp.float32),
     )
     share_weight, share_filters = (
-        lax.psum(part_weight.astype(jnp.bfloat16), "seq").astype(jnp.float32),
+        jnp.sum(lax.all_gather(part_weight.astype(jnp.bfloat16), "seq"), axis=0).astype(
+            jnp.float32
+        ),
         lax.psum(part_filters.astype(jnp.bfloat16), "seq").astype(jnp.float32),
     )
     grad_heads = lax.psum(grad_decay, ("seq", "zero"))

time: 808 us -> 768 us (0.950)
  waiting for transfers between devices: 36.3 us -> 0.07 us
  local copies, waits for them, and re-layouts: 219 us -> 206 us
  blocking collectives: 276 us -> 286 us
    psum x1 -> x0, waiting for transfers between devices: 23.9 us -> none  [per_device(): lax.psum(part_weight.astype(jnp.bfloat16), 'seq').astype(jnp.float32)]
    all_gather x0 -> x1, blocking collectives: none -> 15.6 us  [per_device(): lax.all_gather(part_weight.astype(jnp.bfloat16), 'seq')]
    unnamed x5 -> x4, waiting for transfers between devices: 12.4 us -> 0.04 us
    unnamed x530 -> x490, local copies, waits for them, and re-layouts: 38.1 us -> 37 us
  transfers between devices with their start and end apart: 11 -> 10, of which waited for: 2 -> 0; matrix products, arithmetic and copies ran while one was open for 19% -> 18% of each run, Pallas kernels for 0% -> 0%
where the time goes in v1:
time: 768 us; the launch traced here: 754 us
  blocking collectives  286 us (37%)
  local copies, waits for them, and re-layouts  206 us (27%)
  other arithmetic  139 us (18%)
  matrix products  75 us (10%)
  starting transfers between devices  28.9 us (4%)
  between operations  17.2 us (2%)
    all_gather x12, blocking collectives, prefix(): lax.all_gather(a.astype(kind), axis)  217 us
    slice x6, local copies, waits for them, and re-layouts, conv_core(): ahead_in[KERNEL - 1 - step_back:KERNEL - 1 - step_back + length]  37.2 us
    unnamed x490, local copies, waits for them, and re-layouts  37 us
    psum x1, blocking collectives, per_device(): grad_heads = lax.psum(grad_decay, ('seq', 'zero'))  31.7 us
    ppermute x4, starting transfers between devices, extended(): before = lax.ppermute(last, axis, up)  23.6 us
    add x12, other arithmetic, combine_states(): later[0][..., None, None] * earlier[1] + later[1]  22.9 us
    dot_general x12, matrix products, conv_core(): jnp.einsum('khij,kjhp->kihp', weights, values, preferred_element_type=jnp...  20.9 us
    dot_general x12, matrix products, conv_core(): jnp.einsum('khjn,kjhp->khnp', b_weighted, values, preferred_element_type=...  16.4 us
  transfers between devices with their start and end apart: 10, of which 0 were waited for; matrix products, arithmetic and copies ran while one was open for 18% of the time, Pallas kernels for 0%

profile of v1, /device:TPU:0, one launch (start us, length us, event | category | flops | bytes accessed | tf_op | source)
XLA Modules:
  0.0 753.5 jit_solution(7601086343714934292)
XLA Ops:
  7.2 8.7 %all-gather.14 = bf16[4,320,148]{1,2,0:T(8,128)(2,1)S(1)} all-gather(bf16[1,320,148]{1,2,0:T(8,128)(2,1)} %bitcast.1260), channel_id=1, replica_groups=mesh['grp'=2,'seq'=4,'zero'=4] {'zero'}, dimensions={0}, use_global_device_ids=true | all-gather | bytes 473600 | tf_op jit(solution)/shard_map/all_gather | solution.py:195
  62.7 9.2 %all-gather.6 = bf16[4,1,20,1]{2,3,1,0:T(2,128)(2,1)} all-gather(bf16[1,1,20,1]{2,3,1,0:T(2,128)(2,1)S(1)} %get-tuple-element.1334), channel_id=8, replica_groups=mesh['grp'=2,'seq'=4,'zero'=4] {'seq'}, dimensions={0}, use_global_device_ids=true | all-gather | bytes 200 | tf_op jit(solution)/shard_map/all_gather | solution.py:18
  71.8 8.1 %all-gather.4 = bf16[4,1,20,1]{2,3,1,0:T(2,128)(2,1)} all-gather(bf16[1,1,20,1]{2,3,1,0:T(2,128)(2,1)S(1)} %get-tuple-element.1331), channel_id=6, replica_groups=mesh['grp'=2,'seq'=4,'zero'=4] {'seq'}, dimensions={0}, use_global_device_ids=true | all-gather | bytes 200 | tf_op jit(solution)/shard_map/all_gather | solution.py:18
  80.0 9.2 %all-gather.2 = bf16[4,1,20,1]{2,3,1,0:T(2,128)(2,1)} all-gather(bf16[1,1,20,1]{2,3,1,0:T(2,128)(2,1)S(1)} %get-tuple-element.1328), channel_id=4, replica_groups=mesh['grp'=2,'seq'=4,'zero'=4] {'seq'}, dimensions={0}, use_global_device_ids=true | all-gather | bytes 200 | tf_op jit(solution)/shard_map/all_gather | solution.py:18
  89.2 8.6 %all-gather = bf16[4,1,20,1]{2,3,1,0:T(2,128)(2,1)} all-gather(bf16[1,1,20,1]{2,3,1,0:T(2,128)(2,1)S(1)} %get-tuple-element.1325), channel_id=2, replica_groups=mesh['grp'=2,'seq'=4,'zero'=4] {'seq'}, dimensions={0}, use_global_device_ids=true | all-gather | bytes 200 | tf_op jit(solution)/shard_map/all_gather | solution.py:18
  102.4 6.6 slice.395
  156.9 6.6 slice.366
  174.2 21.0 %all-gather.7 = bf16[80,64,64]{2,1,0:T(8,128)(2,1)} all-gather(bf16[20,64,64]{2,1,0:T(8,128)(2,1)S(1)} %fusion.28), channel_id=9, replica_groups=mesh['grp'=2,'seq'=4,'zero'=4] {'seq'}, dimensions={0}, use_global_device_ids=true | all-gather | bytes 819200 | tf_op jit(solution)/shard_map/all_gather | solution.py:18
  205.1 19.5 %all-gather.11 = bf16[4,20,64,64]{3,2,1,0:T(8,128)(2,1)} all-gather(bf16[1,20,64,64]{3,2,1,0:T(8,128)(2,1)} %copy.689), channel_id=13, replica_groups=mesh['grp'=2,'seq'=4,'zero'=4] {'seq'}, dimensions={0}, use_global_device_ids=true | all-gather | bytes 819200 | tf_op jit(solution)/shard_map/all_gather | solution.py:18
  240.9 23.6 %all-gather.3 = bf16[80,64,64]{2,1,0:T(8,128)(2,1)} all-gather(bf16[20,64,64]{2,1,0:T(8,128)(2,1)S(1)} %fusion.26), channel_id=5, replica_groups=mesh['grp'=2,'seq'=4,'zero'=4] {'seq'}, dimensions={0}, use_global_device_ids=true | all-gather | bytes 819200 | tf_op jit(solution)/shard_map/all_gather | solution.py:18
  265.5 8.5 %while.69 = (s32[]{:T(128)}, f32[1,20,64,64]{3,2,1,0:T(8,128)}, s32[]{:T(128)}, bf16[4,1,20]{2,1,0:T(2,128)(2,1)}, bf16[4,1,20,64,64]{4,3,2,1,0:T(8,128)(2,1)}, ...) while((s32[]{:T(128)}, f32[1,20,64,64]{3,2,1,0:T(8,128)}, s32[]{:T(128)}, bf16[4,1,20]{2,1,0:T(2,128)(2,1)}, ...), condition=%wide.region_5.7_spmd, body=%wide.region_4.6_spmd.sunk | while | flops 245786 | bytes 819555 | solution.py:35
  278.1 19.0 %all-gather.9 = bf16[4,20,64,64]{3,2,1,0:T(8,128)(2,1)} all-gather(bf16[1,20,64,64]{3,2,1,0:T(8,128)(2,1)} %copy.664), channel_id=11, replica_groups=mesh['grp'=2,'seq'=4,'zero'=4] {'seq'}, dimensions={0}, use_global_device_ids=true | all-gather | bytes 819200 | tf_op jit(solution)/shard_map/all_gather | solution.py:18
  341.7 29.2 %all-gather.10 = bf16[4,20,64,64]{3,2,1,0:T(8,128)(2,1)} all-gather(bf16[1,20,64,64]{3,2,1,0:T(8,128)(2,1)} %copy.684), channel_id=12, replica_groups=mesh['grp'=2,'seq'=4,'zero'=4] {'seq'}, dimensions={0}, use_global_device_ids=true | all-gather | bytes 819200 | tf_op jit(solution)/shard_map/all_gather | solution.py:18
  371.8 8.3 %while.74 = (s32[]{:T(128)}, f32[1,20,64,64]{3,2,1,0:T(8,128)}, s32[]{:T(128)}, bf16[4,1,20]{2,1,0:T(2,128)(2,1)}, bf16[4,1,20,64,64]{4,3,2,1,0:T(8,128)(2,1)}, ...) while((s32[]{:T(128)}, f32[1,20,64,64]{3,2,1,0:T(8,128)}, s32[]{:T(128)}, bf16[4,1,20]{2,1,0:T(2,128)(2,1)}, ...), condition=%wide.region_44.46_spmd, body=%wide.region_43.45_spmd.sunk | while | flops 245786 | bytes 819555 | solution.py:35
  394.9 20.7 %all-gather.8 = bf16[4,20,64,64]{3,2,1,0:T(8,128)(2,1)} all-gather(bf16[1,20,64,64]{3,2,1,0:T(8,128)(2,1)} %copy.659), channel_id=10, replica_groups=mesh['grp'=2,'seq'=4,'zero'=4] {'seq'}, dimensions={0}, use_global_device_ids=true | all-gather | bytes 819200 | tf_op jit(solution)/shard_map/all_gather | solution.py:18
  416.5 8.2 %while.72 = (s32[]{:T(128)}, f32[1,20,64,64]{3,2,1,0:T(8,128)}, s32[]{:T(128)}, bf16[4,1,20]{2,1,0:T(2,128)(2,1)}, bf16[4,1,20,64,64]{4,3,2,1,0:T(8,128)(2,1)}, ...) while((s32[]{:T(128)}, f32[1,20,64,64]{3,2,1,0:T(8,128)}, s32[]{:T(128)}, bf16[4,1,20]{2,1,0:T(2,128)(2,1)}, ...), condition=%wide.region_14.16_spmd, body=%wide.region_13.15_spmd.sunk | while | flops 245786 | bytes 819555 | solution.py:35
  429.2 21.7 %all-gather.5 = bf16[80,64,64]{2,1,0:T(8,128)(2,1)} all-gather(bf16[20,64,64]{2,1,0:T(8,128)(2,1)S(1)} %fusion.27), channel_id=7, replica_groups=mesh['grp'=2,'seq'=4,'zero'=4] {'seq'}, dimensions={0}, use_global_device_ids=true | all-gather | bytes 819200 | tf_op jit(solution)/shard_map/all_gather | solution.py:18
  453.2 27.1 %all-gather.1 = bf16[80,64,64]{2,1,0:T(8,128)(2,1)} all-gather(bf16[20,64,64]{2,1,0:T(8,128)(2,1)S(1)} %fusion.25), channel_id=3, replica_groups=mesh['grp'=2,'seq'=4,'zero'=4] {'seq'}, dimensions={0}, use_global_device_ids=true | all-gather | bytes 819200 | tf_op jit(solution)/shard_map/all_gather | solution.py:18
  505.5 8.0 %reverse.8 = f32[1,256,1408]{1,2,0:T(8,128)} reverse(f32[1,256,1408]{1,2,0:T(8,128)S(1)} %bitcast.1188), dimensions={1} | reverse | bytes 2883584
  524.0 12.5 %reverse.9 = f32[1,256,1408]{1,2,0:T(8,128)} reverse(f32[1,256,1408]{1,2,0:T(8,128)} %bitcast.1189), dimensions={1} | reverse | bytes 2883584
  590.5 6.9 collective-permute-start.6
  685.3 31.7 %psum.15 = f32[2,20]{1,0:T(2,128)} all-reduce(f32[2,20]{1,0:T(2,128)S(1)} %maximum_add_fusion), channel_id=1, replica_groups=mesh['grp'=2,'seq'=4,'zero'=4] {'seq','zero'}, use_global_device_ids=true, to_apply=%region_100.102 | all-reduce | flops 40 | bytes 320 | tf_op jit(solution)/shard_map/psum | solution.py:227
  720.0 8.4 %psum.14 = bf16[4,352]{1,0:T(4,128)(2,1)S(1)} all-reduce(bf16[4,352]{1,0:T(4,128)(2,1)S(1)} %copy.719), channel_id=1, replica_groups=mesh['grp'=2,'seq'=4,'zero'=4] {'seq'}, use_global_device_ids=true, to_apply=%region_91.93 | all-reduce | flops 1408 | bytes 5632 | tf_op jit(solution)/shard_map/psum | solution.py:225
  730.1 15.6 %all-gather.15 = bf16[4,320,148]{1,2,0:T(8,128)(2,1)S(1)} all-gather(bf16[1,320,148]{1,2,0:T(8,128)(2,1)S(1)} %bitcast.1257), channel_id=14, replica_groups=mesh['grp'=2,'seq'=4,'zero'=4] {'seq'}, dimensions={0}, use_global_device_ids=true | all-gather | bytes 473600 | tf_op jit(solution)/shard_map/all_gather | solution.py:222
  (817 shorter events, 419.9 us)
Async XLA Ops:
  7.2 711.9 %reduce-scatter.9.cloned.1.call-start = ((), (), s32[]{:S(2)}) async-start(), calls=%async_computation.3 | async-start | bytes 450560
  18.1 106.1 %collective-permute-start.1 = (bf16[1,3,1408]{1,2,0:T(8,128)(2,1)}, bf16[1,3,1408]{1,2,0:T(8,128)(2,1)}, u32[]{:S(2)}, u32[]{:S(2)}) collective-permute-start(bf16[1,3,1408]{1,2,0:T(8,128)(2,1)} %get-tuple-element.1305), channel_id=1, source_target_pairs={{4,0},{8,4},{12,8},{5,1},{9,5},{13,9},{6,2},{10,6},{14,10},{7,3},{... | collective-permute-start | bytes 25352 | tf_op jit(solution)/shard_map/ppermute | solution.py:46
  19.4 104.8 %collective-permute-start = (bf16[1,3,1408]{1,2,0:T(8,128)(2,1)}, bf16[1,3,1408]{1,2,0:T(8,128)(2,1)}, u32[]{:S(2)}, u32[]{:S(2)}) collective-permute-start(bf16[1,3,1408]{1,2,0:T(8,128)(2,1)} %get-tuple-element.1304), channel_id=1, source_target_pairs={{0,4},{4,8},{8,12},{1,5},{5,9},{9,13},{2,6},{6,10},{10,14},{3,7},{... | collective-permute-start | bytes 25352 | tf_op jit(solution)/shard_map/ppermute | solution.py:45
  25.1 72.8 %copy-start.25 = (bf16[1,128,1280]{1,2,0:T(8,128)(2,1)}, bf16[1,128,1280]{1,2,0:T(8,128)(2,1)S(1)}, u32[]{:S(2)}) copy-start(bf16[1,128,1280]{1,2,0:T(8,128)(2,1)S(1)} %rev.50) | copy-start | bytes 983044
  26.6 71.3 %collective-permute-start.3 = (bf16[1,3,1408]{1,2,0:T(8,128)(2,1)}, bf16[1,3,1408]{1,2,0:T(8,128)(2,1)}, u32[]{:S(2)}, u32[]{:S(2)}) collective-permute-start(bf16[1,3,1408]{1,2,0:T(8,128)(2,1)} %get-tuple-element.1307), channel_id=1, source_target_pairs={{4,0},{8,4},{12,8},{5,1},{9,5},{13,9},{6,2},{10,6},{14,10},{7,3},{... | collective-permute-start | bytes 25352 | tf_op jit(solution)/shard_map/ppermute | solution.py:46
  27.8 70.0 %collective-permute-start.2 = (bf16[1,3,1408]{1,2,0:T(8,128)(2,1)}, bf16[1,3,1408]{1,2,0:T(8,128)(2,1)}, u32[]{:S(2)}, u32[]{:S(2)}) collective-permute-start(bf16[1,3,1408]{1,2,0:T(8,128)(2,1)} %get-tuple-element.1306), channel_id=1, source_target_pairs={{0,4},{4,8},{8,12},{1,5},{5,9},{9,13},{2,6},{6,10},{10,14},{3,7},{... | collective-permute-start | bytes 25352 | tf_op jit(solution)/shard_map/ppermute | solution.py:45
  33.6 23.7 %copy-start.52 = (f32[1,1,128,20]{3,2,1,0:T(8,128)}, f32[1,1,128,20]{3,2,1,0:T(8,128)S(1)}, u32[]{:S(2)}) copy-start(f32[1,1,128,20]{3,2,1,0:T(8,128)S(1)} %reduce_window_sum.90) | copy-start | bytes 30724
  35.9 24.7 %copy-start.54 = (f32[1,1,128,20]{3,2,1,0:T(8,128)}, f32[1,1,128,20]{3,2,1,0:T(8,128)S(1)}, u32[]{:S(2)}) copy-start(f32[1,1,128,20]{3,2,1,0:T(8,128)S(1)} %reduce_window_sum.86) | copy-start | bytes 30724
  38.7 22.6 %copy-start.58 = (f32[1,1,128,20]{3,2,1,0:T(8,128)}, f32[1,1,128,20]{3,2,1,0:T(8,128)S(1)}, u32[]{:S(2)}) copy-start(f32[1,1,128,20]{3,2,1,0:T(8,128)S(1)} %reduce_window_sum.84) | copy-start | bytes 30724
  45.3 80.6 %copy-start.134 = (f32[1408]{0:T(1024)}, f32[1408]{0:T(1024)S(1)}, u32[]{:S(2)}) copy-start(f32[1408]{0:T(1024)S(1)} %get-tuple-element.1150) | copy-start | bytes 16900
  45.3 80.6 %copy-start.136 = (f32[1408]{0:T(1024)}, f32[1408]{0:T(1024)S(1)}, u32[]{:S(2)}) copy-start(f32[1408]{0:T(1024)S(1)} %get-tuple-element.1151) | copy-start | bytes 16900
  200.8 23.8 %copy-start.2 = (f32[1,20,64,64]{3,2,1,0:T(8,128)}, f32[1,20,64,64]{3,2,1,0:T(8,128)S(1)}, u32[]{:S(2)}) copy-start(f32[1,20,64,64]{3,2,1,0:T(8,128)S(1)} %get-tuple-element.760) | copy-start | bytes 983044
  587.9 27.3 %copy-start.59 = (f32[1,1,128,20]{3,2,1,0:T(8,128)S(1)}, f32[1,1,128,20]{3,2,1,0:T(8,128)}, u32[]{:S(2)}) copy-start(f32[1,1,128,20]{3,2,1,0:T(8,128)} %copy-done.58) | copy-start | bytes 30724
  588.0 27.3 %copy-start.109 = (f32[1,128,148]{2,1,0:T(8,128)S(1)}, f32[1,128,148]{2,1,0:T(8,128)}, u32[]{:S(2)}) copy-start(f32[1,128,148]{2,1,0:T(8,128)} %copy-done.108) | copy-start | bytes 227332
  588.0 27.3 %copy-start.195 = (f32[20]{0:T(128)S(1)}, f32[20]{0:T(128)}, u32[]{:S(2)}) copy-start(f32[20]{0:T(128)} %get-tuple-element.1326) | copy-start | bytes 244
  589.0 25.0 %copy-start.133 = (f32[1,1,128,20]{3,2,1,0:T(8,128)S(1)}, f32[1,1,128,20]{3,2,1,0:T(8,128)}, u32[]{:S(2)}) copy-start(f32[1,1,128,20]{3,2,1,0:T(8,128)} %get-tuple-element.1367) | copy-start | bytes 30724
  589.0 27.6 %copy-start.57 = (f32[1,1,128,20]{3,2,1,0:T(8,128)S(1)}, f32[1,1,128,20]{3,2,1,0:T(8,128)}, u32[]{:S(2)}) copy-start(f32[1,1,128,20]{3,2,1,0:T(8,128)} %copy-done.56) | copy-start | bytes 30724
  589.0 27.6 %copy-start.103 = (f32[1,128,148]{2,1,0:T(8,128)S(1)}, f32[1,128,148]{2,1,0:T(8,128)}, u32[]{:S(2)}) copy-start(f32[1,128,148]{2,1,0:T(8,128)} %copy-done.102) | copy-start | bytes 227332
  589.1 61.9 %collective-permute-start.7 = (bf16[1,3,1408]{1,2,0:T(8,128)(2,1)}, bf16[1,3,1408]{1,2,0:T(8,128)(2,1)}, u32[]{:S(2)}, u32[]{:S(2)}) collective-permute-start(bf16[1,3,1408]{1,2,0:T(8,128)(2,1)} %get-tuple-element.1271), channel_id=1, source_target_pairs={{4,0},{8,4},{12,8},{5,1},{9,5},{13,9},{6,2},{10,6},{14,10},{7,3},{... | collective-permute-start | bytes 25352 | tf_op jit(solution)/shard_map/ppermute | solution.py:46
  590.5 60.5 %collective-permute-start.6 = (bf16[1,3,1408]{1,2,0:T(8,128)(2,1)}, bf16[1,3,1408]{1,2,0:T(8,128)(2,1)}, u32[]{:S(2)}, u32[]{:S(2)}) collective-permute-start(bf16[1,3,1408]{1,2,0:T(8,128)(2,1)} %get-tuple-element.1270), channel_id=1, source_target_pairs={{0,4},{4,8},{8,12},{1,5},{5,9},{9,13},{2,6},{6,10},{10,14},{3,7},{... | collective-permute-start | bytes 25352 | tf_op jit(solution)/shard_map/ppermute | solution.py:45
  605.2 62.0 %collective-permute-start.5 = (bf16[1,3,1408]{1,2,0:T(8,128)(2,1)}, bf16[1,3,1408]{1,2,0:T(8,128)(2,1)}, u32[]{:S(2)}, u32[]{:S(2)}) collective-permute-start(bf16[1,3,1408]{1,2,0:T(8,128)(2,1)} %get-tuple-element.1269), channel_id=1, source_target_pairs={{4,0},{8,4},{12,8},{5,1},{9,5},{13,9},{6,2},{10,6},{14,10},{7,3},{... | collective-permute-start | bytes 25352 | tf_op jit(solution)/shard_map/ppermute | solution.py:46
  606.5 60.7 %collective-permute-start.4 = (bf16[1,3,1408]{1,2,0:T(8,128)(2,1)}, bf16[1,3,1408]{1,2,0:T(8,128)(2,1)}, u32[]{:S(2)}, u32[]{:S(2)}) collective-permute-start(bf16[1,3,1408]{1,2,0:T(8,128)(2,1)} %get-tuple-element.1268), channel_id=1, source_target_pairs={{0,4},{4,8},{8,12},{1,5},{5,9},{9,13},{2,6},{6,10},{10,14},{3,7},{... | collective-permute-start | bytes 25352 | tf_op jit(solution)/shard_map/ppermute | solution.py:45
  638.5 90.5 %reduce-scatter.7.cloned.1.call-start = ((), (), s32[]{:S(2)}) async-start(), calls=%async_computation.2 | async-start | bytes 819200
  683.7 33.4 %copy-start.24 = (bf16[1280,148]{0,1:T(8,128)(2,1)S(1)}, bf16[1280,148]{0,1:T(8,128)(2,1)}, u32[]{:S(2)}) copy-start(bf16[1280,148]{0,1:T(8,128)(2,1)} %copy-done.23) | copy-start | bytes 1136644
  (225 other events, 1192.5 us)
Sparse Core Ops, SparseCore 0:
  638.6 24.8 reduce-scatter.8
  685.3 26.7 reduce-scatter.6
